TPU v7x, 32 devices: a whole 2x2x4 slice. The times are simulated.
32 devices in a mesh: seq: 8 (over y, x, core), row: 4 (over z).
Axes of the slice: x: 2, y: 2, z: 4, core: 2. Of those that a mesh axis runs over, the one named last changes fastest.
Arguments:
- tokens: bfloat16 [32, 1024, 768], P('row', 'seq'), may hold values from -6 to 6
- segment_ids: int32 [32, 1024], P('row'), may hold values from 0 to 1023, as said below
- w_in: bfloat16 [768, 3840], replicated, may hold values from -0.21875 to 0.21875
- w_out: bfloat16 [768, 768], replicated, may hold values from -3 to 3
- w_up: bfloat16 [768, 3072], replicated, may hold values from -0.21875 to 0.21875
- w_down: bfloat16 [3072, 768], replicated, may hold values from -0.109375 to 0.109375
- conv_kernel: float32 [5, 768], replicated, may hold values from -2.5 to 2.5
- norm_gain: float32 [2, 768], replicated, may hold values from 0.5 to 1.5
- norm_bias: float32 [2, 768], replicated, may hold values from -1.5 to 1.5
- cotangent: bfloat16 [32, 1024, 768], P('row', 'seq'), may hold values from -6 to 6
Outputs:
- layer_out: bfloat16 [32, 1024, 768], P('row', 'seq')
- token_grad: float32 [32, 1024, 768], P('row', 'seq')
- w_in_grad: float32 [768, 3840], P('seq', 'row')
- w_out_grad: float32 [768, 768], P('seq', 'row')
- w_up_grad: float32 [768, 3072], P('seq', 'row')
- w_down_grad: float32 [3072, 768], P('seq', 'row')
- conv_kernel_grad: float32 [5, 768], replicated
- norm_gain_grad: float32 [2, 768], replicated
- norm_bias_grad: float32 [2, 768], replicated
Inputs may be any that keep to these rules, and one draw needn't show every extreme that they name: `segment_ids`: each token's id is the position in its row at which its document begins, so ids never fall along a row and equal ids mark one document.
All inputs are finite; a program needn't handle non-finite values.
Results may differ from a plain program's by a relative error of at most 0.015.
Values may be sent and summed in bfloat16 or wider, within the bound.
A program may use at most 384 MiB of HBM per device.

v0:
```python
import jax
import jax.numpy as jnp
from jax import lax
from jax.sharding import PartitionSpec as P

HEADS = 12
HEAD = 64
WIN = 128
KER = 5
STR = 4


EPSILON = 1e-05
ROOT_HALF = 0.7071067811865476
NEG_LARGE = -1e30


def with_halo(x, sides, width):
    for axis, dim in sides:
        count, length = (lax.axis_size(axis), x.shape[dim])
        up = [(i, (i + 1) % count) for i in range(count - 1)]
        down = [(j, i) for i, j in up]
        last = lax.slice_in_dim(x, length - width, length, axis=dim)
        leading = lax.slice_in_dim(x, 0, width, axis=dim)
        before = lax.ppermute(last, axis, up)
        after = lax.ppermute(leading, axis, down)
        x = jnp.concatenate([before, x, after], axis=dim)
    return x


def passed_along(block, axis, distance):
    devices = range(lax.axis_size(axis))
    route = [(i - distance, i) for i in devices if i - distance in devices]
    return lax.ppermute(block, axis, route)


def layer_norm(values, gain_row, offset):
    centred = values - jnp.mean(values, axis=-1, keepdims=True)
    spread = jnp.mean(centred * centred, axis=-1, keepdims=True)
    return centred * lax.rsqrt(spread + EPSILON) * gain_row + offset


def gelu_exact(values):
    return 0.5 * values * (1.0 + jax.scipy.special.erf(values * ROOT_HALF))


def pool_taps(extended, kernel, tap_mask):
    batch_rows = extended.shape[0]
    feat_width = extended.shape[2]
    pooled_len = tap_mask.shape[1]
    summed = jnp.zeros((batch_rows, pooled_len, feat_width), jnp.float32)
    for tap_index in range(KER):
        tap_rows = extended[:, tap_index : tap_index + pooled_len * STR]
        tap_rows = tap_rows.reshape(batch_rows, pooled_len, STR, feat_width)[:, :, 0]
        summed = summed + tap_rows * kernel[tap_index] * tap_mask[:, :, tap_index : tap_index + 1]
    return summed


def split_heads(values):
    return values.reshape(values.shape[0], values.shape[1], HEADS, HEAD)


def masked_scores(query_heads, key_rows, allowed, head_scale):
    scores = jnp.einsum(
        "rqhd,rkhd->rhqk", query_heads, split_heads(key_rows), preferred_element_type=jnp.float32
    )
    return jnp.where(allowed[:, None], scores * head_scale, NEG_LARGE)


def tile_order(grad, seq_count, row_count):
    first, second = grad.shape
    tiles = grad.reshape(seq_count, first // seq_count, row_count, second // row_count)
    tiles = tiles.transpose(1, 0, 2, 3)
    return tiles.reshape(first // seq_count, seq_count * second)


def body(
    tokens, segment_ids, w_in, w_out, w_up, w_down, conv_kernel, norm_gain, norm_bias, cotangent
):
    batch_rows, shard_len, model_width = tokens.shape
    half_win = WIN // 2
    edge_len = KER // 2
    pooled_local = shard_len // STR
    head_scale = HEAD ** (-0.5)
    token_count = batch_rows * shard_len
    seq_start = lax.axis_index("seq") * shard_len
    flat_tokens = tokens.reshape(token_count, model_width)
    own_seg = lax.dynamic_slice_in_dim(segment_ids, seq_start, shard_len, 1)
    padded_seg = jnp.pad(segment_ids, ((0, 0), (half_win, half_win)), constant_values=-1)
    window_seg = lax.dynamic_slice_in_dim(padded_seg, seq_start, shard_len + 2 * half_win, 1)
    far_seg = segment_ids[:, ::STR]
    conv_pad = jnp.pad(segment_ids, ((0, 0), (edge_len, edge_len)), constant_values=-1)
    conv_seg = lax.dynamic_slice_in_dim(conv_pad, seq_start, shard_len + 2 * edge_len, 1)
    centre_seg = own_seg[:, ::STR]
    tap_mask = jnp.stack(
        [
            conv_seg[:, tap_index : tap_index + shard_len].reshape(batch_rows, pooled_local, STR)[
                :, :, 0
            ]
            == centre_seg
            for tap_index in range(KER)
        ],
        axis=-1,
    ).astype(jnp.float32)
    offsets = jnp.arange(shard_len + 2 * half_win)[None, :] - jnp.arange(shard_len)[:, None]
    near_allowed = ((offsets >= 0) & (offsets <= 2 * half_win))[None] & (
        own_seg[:, :, None] == window_seg[:, None, :]
    )
    far_allowed = own_seg[:, :, None] == far_seg[:, None, :]
    projected = jnp.dot(flat_tokens, w_in[:, : 3 * model_width], preferred_element_type=jnp.float32)
    projected = projected.astype(jnp.bfloat16).reshape(batch_rows, shard_len, 3 * model_width)
    queries = projected[..., :model_width]
    near_kv = projected[..., model_width:]
    window_kv = with_halo(near_kv, (("seq", 1),), half_win)
    left_rim = passed_along(tokens[:, shard_len - edge_len :], "seq", 1)
    extended = jnp.concatenate(
        [left_rim, tokens, jnp.zeros((batch_rows, edge_len, model_width), jnp.bfloat16)], axis=1
    ).astype(jnp.float32)
    pooled_x, pool_back = jax.vjp(
        lambda ext_in, kernel_in: pool_taps(ext_in, kernel_in, tap_mask), extended, conv_kernel
    )
    pooled_low = pooled_x.astype(jnp.bfloat16).reshape(batch_rows * pooled_local, model_width)
    far_kv = jnp.dot(pooled_low, w_in[:, 3 * model_width :], preferred_element_type=jnp.float32)
    far_kv = far_kv.astype(jnp.bfloat16).reshape(batch_rows, pooled_local, 2 * model_width)
    far_all = lax.all_gather(far_kv, "seq", axis=1, tiled=True)
    query_heads = split_heads(queries)
    near_keys = window_kv[..., :model_width]
    near_values = split_heads(window_kv[..., model_width:])
    near_scores = masked_scores(query_heads, near_keys, near_allowed, head_scale)
    far_scores = masked_scores(query_heads, far_all[..., :model_width], far_allowed, head_scale)
    row_top = jnp.maximum(
        jnp.max(near_scores, axis=-1, keepdims=True), jnp.max(far_scores, axis=-1, keepdims=True)
    )
    near_exp = jnp.exp(near_scores - row_top)
    far_exp = jnp.exp(far_scores - row_top)
    row_total = jnp.sum(near_exp, axis=-1, keepdims=True) + jnp.sum(far_exp, axis=-1, keepdims=True)
    log_total = row_top + jnp.log(row_total)
    near_prob = near_exp / row_total
    near_weight = near_prob.astype(jnp.bfloat16)
    far_weight = (far_exp / row_total).astype(jnp.bfloat16)
    mixed = jnp.einsum(
        "rhqk,rkhd->rqhd", near_weight, near_values, preferred_element_type=jnp.float32
    )
    mixed = mixed + jnp.einsum(
        "rhqk,rkhd->rqhd",
        far_weight,
        split_heads(far_all[..., model_width:]),
        preferred_element_type=jnp.float32,
    )
    attended = mixed.reshape(token_count, model_width).astype(jnp.bfloat16)
    attn_proj = jnp.dot(attended, w_out, preferred_element_type=jnp.float32)
    resid_one = flat_tokens.astype(jnp.float32) + attn_proj
    normed_one, norm_one_back = jax.vjp(layer_norm, resid_one, norm_gain[0], norm_bias[0])
    normed_low = normed_one.astype(jnp.bfloat16)
    up_value = jnp.dot(normed_low, w_up, preferred_element_type=jnp.float32)
    gelu_value, gelu_back = jax.vjp(gelu_exact, up_value)
    activated = gelu_value.astype(jnp.bfloat16)
    down_value = jnp.dot(activated, w_down, preferred_element_type=jnp.float32)
    resid_two = normed_one + down_value
    output_full, norm_two_back = jax.vjp(layer_norm, resid_two, norm_gain[1], norm_bias[1])
    layer_out = output_full.astype(jnp.bfloat16).reshape(batch_rows, shard_len, model_width)
    out_grad = cotangent.reshape(token_count, model_width).astype(jnp.float32)
    resid_two_grad, gain_two_grad, bias_two_grad = norm_two_back(out_grad)
    resid_two_low = resid_two_grad.astype(jnp.bfloat16)
    w_down_grad = jnp.dot(activated.T, resid_two_low, preferred_element_type=jnp.float32)
    act_grad = jnp.einsum("tk,fk->tf", resid_two_low, w_down, preferred_element_type=jnp.float32)
    up_low = gelu_back(act_grad)[0].astype(jnp.bfloat16)
    w_up_grad = jnp.dot(normed_low.T, up_low, preferred_element_type=jnp.float32)
    normed_grad = resid_two_grad + jnp.einsum(
        "tf,df->td", up_low, w_up, preferred_element_type=jnp.float32
    )
    resid_one_grad, gain_one_grad, bias_one_grad = norm_one_back(normed_grad)
    resid_one_low = resid_one_grad.astype(jnp.bfloat16)
    w_out_grad = jnp.dot(attended.T, resid_one_low, preferred_element_type=jnp.float32)
    attended_grad = jnp.einsum(
        "tk,dk->td", resid_one_low, w_out, preferred_element_type=jnp.float32
    )
    grad_heads = split_heads(
        attended_grad.astype(jnp.bfloat16).reshape(batch_rows, shard_len, model_width)
    )
    far_back = lax.all_gather(far_kv, "seq", axis=1, tiled=True)
    far_key_heads = split_heads(far_back[..., :model_width])
    far_value_heads = split_heads(far_back[..., model_width:])
    far_prob = jnp.exp(
        masked_scores(query_heads, far_back[..., :model_width], far_allowed, head_scale) - log_total
    )
    far_prob_low = far_prob.astype(jnp.bfloat16)
    near_dprob = jnp.einsum(
        "rqhd,rkhd->rhqk", grad_heads, near_values, preferred_element_type=jnp.float32
    )
    far_dprob = jnp.einsum(
        "rqhd,rkhd->rhqk", grad_heads, far_value_heads, preferred_element_type=jnp.float32
    )
    row_dot = jnp.sum(near_prob * near_dprob, axis=-1, keepdims=True) + jnp.sum(
        far_prob * far_dprob, axis=-1, keepdims=True
    )
    near_dscore = (near_prob * (near_dprob - row_dot)).astype(jnp.bfloat16)
    far_dscore = (far_prob * (far_dprob - row_dot)).astype(jnp.bfloat16)
    query_grad = jnp.einsum(
        "rhqk,rkhd->rqhd", near_dscore, split_heads(near_keys), preferred_element_type=jnp.float32
    )
    query_grad = (
        query_grad
        + jnp.einsum(
            "rhqk,rkhd->rqhd", far_dscore, far_key_heads, preferred_element_type=jnp.float32
        )
    ) * head_scale
    near_key_grad = (
        jnp.einsum("rhqk,rqhd->rkhd", near_dscore, query_heads, preferred_element_type=jnp.float32)
        * head_scale
    )
    near_value_grad = jnp.einsum(
        "rhqk,rqhd->rkhd", near_weight, grad_heads, preferred_element_type=jnp.float32
    )
    far_count = far_back.shape[1]
    far_key_grad = (
        jnp.einsum("rhqk,rqhd->rkhd", far_dscore, query_heads, preferred_element_type=jnp.float32)
        * head_scale
    )
    far_value_grad = jnp.einsum(
        "rhqk,rqhd->rkhd", far_prob_low, grad_heads, preferred_element_type=jnp.float32
    )
    far_terms = jnp.concatenate(
        [
            far_key_grad.reshape(batch_rows, far_count, model_width),
            far_value_grad.reshape(batch_rows, far_count, model_width),
        ],
        axis=-1,
    )
    far_grad = lax.psum_scatter(
        far_terms.astype(jnp.bfloat16), "seq", scatter_dimension=1, tiled=True
    )
    near_len = shard_len + 2 * half_win
    near_terms = jnp.concatenate(
        [
            near_key_grad.reshape(batch_rows, near_len, model_width),
            near_value_grad.reshape(batch_rows, near_len, model_width),
        ],
        axis=-1,
    )
    from_right = passed_along(near_terms[:, :half_win].astype(jnp.bfloat16), "seq", -1).astype(
        jnp.float32
    )
    from_left = passed_along(
        near_terms[:, shard_len + half_win :].astype(jnp.bfloat16), "seq", 1
    ).astype(jnp.float32)
    near_grad = near_terms[:, half_win : shard_len + half_win]
    near_grad = near_grad + jnp.pad(from_left, ((0, 0), (0, shard_len - half_win), (0, 0)))
    near_grad = near_grad + jnp.pad(from_right, ((0, 0), (shard_len - half_win, 0), (0, 0)))
    proj_grad = jnp.concatenate(
        [query_grad.reshape(batch_rows, shard_len, model_width), near_grad], axis=-1
    )
    proj_grad = proj_grad.astype(jnp.bfloat16).reshape(token_count, 3 * model_width)
    w_in_near_grad = jnp.dot(flat_tokens.T, proj_grad, preferred_element_type=jnp.float32)
    far_low = far_grad.reshape(batch_rows * pooled_local, 2 * model_width)
    w_in_far_grad = jnp.dot(pooled_low.T, far_low, preferred_element_type=jnp.float32)
    pooled_grad = jnp.einsum(
        "tk,dk->td", far_low, w_in[:, 3 * model_width :], preferred_element_type=jnp.float32
    )
    extended_grad, kernel_grad = pool_back(
        pooled_grad.reshape(batch_rows, pooled_local, model_width)
    )
    rim_back = passed_along(extended_grad[:, :edge_len].astype(jnp.bfloat16), "seq", -1).astype(
        jnp.float32
    )
    token_grad = resid_one_grad + jnp.einsum(
        "tk,dk->td", proj_grad, w_in[:, : 3 * model_width], preferred_element_type=jnp.float32
    )
    token_grad = (
        token_grad.reshape(batch_rows, shard_len, model_width)
        + extended_grad[:, edge_len : edge_len + shard_len]
    )
    token_grad = token_grad + jnp.pad(rim_back, ((0, 0), (shard_len - edge_len, 0), (0, 0)))
    w_in_grad = jnp.concatenate([w_in_near_grad, w_in_far_grad], axis=1)
    small_stack = jnp.concatenate(
        [kernel_grad, jnp.stack([gain_one_grad, gain_two_grad, bias_one_grad, bias_two_grad])],
        axis=0,
    )
    small_sum = lax.psum(small_stack, ("seq", "row"))
    seq_count = lax.axis_size("seq")
    row_count = lax.axis_size("row")
    summed = (
        lax.psum_scatter(
            tile_order(w_in_grad, seq_count, row_count),
            ("seq", "row"),
            scatter_dimension=1,
            tiled=True,
        ),
        lax.psum_scatter(
            tile_order(w_out_grad, seq_count, row_count),
            ("seq", "row"),
            scatter_dimension=1,
            tiled=True,
        ),
        lax.psum_scatter(
            tile_order(w_up_grad, seq_count, row_count),
            ("seq", "row"),
            scatter_dimension=1,
            tiled=True,
        ),
        lax.psum_scatter(
            tile_order(w_down_grad, seq_count, row_count),
            ("seq", "row"),
            scatter_dimension=1,
            tiled=True,
        ),
    )
    return (
        layer_out,
        token_grad,
        summed[0],
        summed[1],
        summed[2],
        summed[3],
        small_sum[:KER],
        small_sum[KER : KER + 2],
        small_sum[KER + 2 : KER + 4],
    )


def solution(mesh):
    placed = (
        P("row", "seq", None),
        P("row", None),
        P(),
        P(),
        P(),
        P(),
        P(),
        P(),
        P(),
        P("row", "seq", None),
    )
    return jax.shard_map(
        body,
        mesh=mesh,
        in_specs=placed,
        out_specs=(
            P("row", "seq", None),
            P("row", "seq", None),
            P("seq", "row"),
            P("seq", "row"),
            P("seq", "row"),
            P("seq", "row"),
            P(),
            P(),
            P(),
        ),
        check_vma=False,
    )
```

profile of v0, /device:TPU:0, one launch (start us, length us, event | category | flops | bytes accessed | tf_op | source)
XLA Modules:
  0.0 962.8 jit_solution(14835006625779334062)
XLA Ops:
  16.6 11.5 %fusion.123 = (f32[8,128,768]{2,0,1:T(8,128)}, f32[8,128,768]{2,0,1:T(8,128)}, f32[8,128,768]{2,0,1:T(8,128)}, f32[8,128,768]{2,0,1:T(8,128)}, f32[8,128,768]{2,0,1:T(8,128)}) fusion(f32[8,132,768]{2,0,1:T(8,128)} %maximum_convert_fusion), kind=kLoop, calls=%fused_computation.222 | loop fusion | bytes 31457280 | tf_op jit(solution)/shard_map/jvp()/slice | solution.py:53
  40.7 6.0 convolution_convert_fusion
  49.8 5.8 collective-permute-start
  82.9 8.9 fusion.1
  91.9 16.9 %all-gather.2.cloned.1.call-done = bf16[8,256,1536]{2,1,0:T(8,128)(2,1)} async-done(((bf16[8,32,1536]{2,1,0:T(8,128)(2,1)}), bf16[8,256,1536]{2,1,0:T(8,128)(2,1)}) %all-gather.2.cloned.1.call-update) | async-done | bytes 6291472 | tf_op jit(solution)/shard_map/all_gather | solution.py:125
  108.8 6.1 fusion.121
  124.2 5.3 fusion.21
  129.5 12.7 %fusion.2 = (f32[8,12,128]{2,1,0:T(8,128)S(1)}, f32[8,12,128]{2,1,0:T(8,128)S(1)}) fusion(f32[8,12,128]{2,1,0:T(8,128)S(1)} %max.11, f32[8,12,128,256]{3,2,1,0:T(8,128)S(1)} %get-tuple-element.112, pred[8,128,256]{2,1,0:T(8,128)(4,1)S(1)} %get-tuple-element.107, f32[8,12,128,256]{3,2,1,0:T(8,128)} %get-tuple-element.110, ...), kind=kLoop, calls=%fused_computation.19 | loop fusion | flops 25141248 | bytes 25837568 | tf_op jit(solution)/shard_map/reduce_sum | solution.py:136
  142.3 5.9 fusion.13
  148.3 7.6 fusion.48
  160.4 8.7 multiply_convert_fusion.2
  169.1 5.4 fusion.126
  180.3 17.9 %add_convert_fusion = bf16[1024,3072]{1,0:T(8,128)(2,1)S(1)} fusion(f32[1024,3072]{1,0:T(8,128)} %get-tuple-element.116, bf16[3072,768]{1,0:T(8,128)(2,1)S(1)} %bitcast.376, f32[1024,768]{1,0:T(8,128)S(1)} %get-tuple-element.60, f32[1024]{0:T(1024)S(1)} %negate_multiply_fusion.1), kind=kOutput, calls=%fused_computation.9 | convolution fusion | flops 4874305536 | bytes 26742784 | tf_op jit(solution)/shard_map/tk,fk->tf/dot_general | solution.py:166
  198.2 11.3 %multiply_reduce_fusion.2 = (f32[768]{0:T(1024)}, f32[1024]{0:T(1024)S(1)}, f32[768]{0:T(1024)}, f32[1024,768]{1,0:T(8,128)S(1)}) fusion(f32[1024,768]{1,0:T(8,128)S(1)} %get-tuple-element.114, f32[1024]{0:T(1024)S(1)} %fusion.96, f32[1024]{0:T(1024)S(1)} %broadcast_multiply_fusion.2, f32[768]{0:T(1024)S(1)} %get-tuple-element.124, ...), kind=kOutput, calls=%fused_computation.56 | convolution fusion | flops 4839699456 | bytes 20472832 | tf_op jit(solution)/shard_map/tf,df->td/dot_general | solution.py:169
  218.7 7.5 fusion.37
  226.3 12.0 %multiply_reduce_fusion = (f32[8,12,128]{2,1,0:T(8,128)S(1)}, f32[8,12,128,256]{3,2,1,0:T(8,128)}) fusion(f32[8,12,128]{2,1,0:T(8,128)S(1)} %get-tuple-element.61, f32[8,12,128,256]{3,2,1,0:T(8,128)} %copy-done.2, pred[8,128,256]{2,1,0:T(8,128)(4,1)S(1)} %get-tuple-element.107, bf16[8,256,12,64]{1,3,2,0:T(8,128)(2,1)} %bitcast.333, ...), kind=kOutput, calls=%fused_computation.6 | convolution fusion | flops 418369536 | bytes 30244864 | tf_op jit(solution)/shard_map/rqhd,rkhd->rhqk/dot_general | solution.py:191
  238.3 11.2 %multiply_reduce_fusion.1 = (f32[8,12,128]{2,1,0:T(8,128)S(1)}, f32[8,12,128,256]{3,2,1,0:T(8,128)}) fusion(f32[8,12,128]{2,1,0:T(8,128)S(1)} %get-tuple-element.62, f32[8,12,128]{2,1,0:T(8,128)S(1)} %max.11, f32[8,12,128,256]{3,2,1,0:T(8,128)S(1)} %bitcast.305, pred[8,128,256]{2,1,0:T(8,128)(4,1)S(1)} %get-tuple-element.108, ...), kind=kOutput, calls=%fused_computation.8 | convolution fusion | flops 421515264 | bytes 30294016 | tf_op jit(solution)/shard_map/rqhd,rkhd->rhqk/dot_general | solution.py:188
  254.1 21.9 %multiply_convert_fusion.1 = (bf16[8,12,128,256]{3,2,1,0:T(8,128)(2,1)}, bf16[8,12,128,256]{3,2,1,0:T(8,128)(2,1)S(1)}) fusion(f32[8,12,128,256]{3,2,1,0:T(8,128)} %get-tuple-element.121, f32[8,12,128]{2,1,0:T(8,128)S(1)} %add.213, f32[8,12,128]{2,1,0:T(8,128)S(1)} %get-tuple-element.62, f32[8,12,128]{2,1,0:T(8,128)S(1)} %max.11, ...), kind=kLoop, calls=%fused_computation.5 | loop fusion | flops 40894464 | bytes 63635456 | tf_op jit(solution)/shard_map/convert_element_type | solution.py:197
  284.2 5.9 pad_maximum_fusion.3
  297.4 6.6 broadcast_multiply_fusion
  304.0 9.7 %fusion.27 = f32[8,12,64,256]{3,2,1,0:T(8,128)} fusion(bf16[8,128,12,64]{1,0,3,2:T(8,128)(2,1)S(1)} %bitcast.346, f32[8,12,128,256]{3,2,1,0:T(8,128)} %get-tuple-element.110, f32[8,12,128]{2,1,0:T(8,128)S(1)} %get-tuple-element.62, f32[8,12,128]{2,1,0:T(8,128)S(1)} %max.11, pred[8,128,256]{2,1,0:T(8,128)(4,1)S(1)} %get-tuple-element.108), kind=kOutput, calls=%fused_computation.65 | convolution fusion | flops 418381824 | bytes 20807680 | tf_op jit(solution)/shard_map/rhqk,rqhd->rkhd/dot_general | solution.py:212
  313.7 8.0 fusion
  321.7 6.9 fusion.119
  339.0 33.9 %collective-permute-start.3 = (bf16[8,64,1536]{2,1,0:T(8,128)(2,1)}, bf16[8,64,1536]{2,1,0:T(8,128)(2,1)}, u32[]{:S(2)}, u32[]{:S(2)}) collective-permute-start(bf16[8,64,1536]{2,1,0:T(8,128)(2,1)} %copy.180), channel_id=1, source_target_pairs={{0,4},{4,8},{8,12},{12,16},{16,20},{20,24},{24,28},{1,5},{5,9},{9,... | collective-permute-start | bytes 4718600 | tf_op jit(solution)/shard_map/ppermute | solution.py:34
  372.8 4.9 convolution_bitcast_fusion.2
  381.8 6.2 fusion.129
  388.0 6.2 multiply_convert_fusion.4
  402.5 8.4 fusion.11
  412.7 7.0 convolution_bitcast_fusion
  419.9 5.9 convolution_bitcast_fusion.1
  425.7 9.8 %pad_maximum_fusion.1 = f32[768,3840]{0,1:T(8,128)} fusion(f32[768,1536]{0,1:T(8,128)} %convolution_bitcast_fusion.1, f32[768,2304]{0,1:T(8,128)} %convolution_bitcast_fusion), kind=kLoop, calls=%fused_computation.17 | loop fusion | flops 2949120 | bytes 23592960 | tf_op jit(solution)/shard_map/concatenate | solution.py:274
  435.5 12.5 %copy.196 = f32[768,3840]{1,0:T(8,128)} copy(f32[768,3840]{0,1:T(8,128)} %pad_maximum_fusion.1) | data formatting | bytes 23592960 | tf_op jit(solution)/shard_map/concatenate | solution.py:274
  448.0 16.9 %reshape.344 = f32[8,96,4,960]{3,2,1,0:T(4,128)} reshape(f32[768,3840]{1,0:T(8,128)} %copy.196) | data formatting | bytes 23592960 | tf_op jit(solution)/shard_map/reshape | solution.py:72
  464.9 17.6 %copy.212 = f32[96,8,4,960]{0,3,2,1:T(8,128)} copy(f32[96,8,4,960]{3,2,0,1:T(4,128)} %bitcast.313) | data formatting | bytes 23592960
  483.2 11.2 %fusion.109 = f32[3072,768]{0,1:T(8,128)} fusion(bf16[1024,3072]{1,0:T(8,128)(2,1)} %copy-done.70, f32[1024,768]{1,0:T(8,128)} %copy-done.31, f32[1024]{0:T(1024)S(1)} %copy-done.69), kind=kOutput, calls=%fused_computation.212 | convolution fusion | flops 4833411072 | bytes 18878464 | tf_op jit(solution)/shard_map/dot_general | solution.py:165
  494.4 5.9 copy.235
  500.2 5.3 copy.202
  506.2 11.8 %fusion.111 = f32[768,3072]{1,0:T(8,128)} fusion(bf16[1024,3072]{1,0:T(8,128)(2,1)} %copy-done.24, f32[1024,768]{1,0:T(8,128)} %copy-done.6, f32[768]{0:T(1024)S(1)} %copy-done.54, f32[768]{0:T(1024)S(1)} %copy-done.52, f32[1024]{0:T(1024)S(1)} %copy-done.39, f32[1024]{0:T(1024)S(1)} %copy-done.37), kind=kOutput, calls=%fused_computation.214 | convolution fusion | flops 4835770368 | bytes 18888704 | tf_op jit(solution)/shard_map/dot_general | solution.py:168
  518.0 12.9 %reshape.347 = f32[8,96,4,768]{3,2,1,0:T(4,128)} reshape(f32[768,3072]{1,0:T(8,128)} %fusion.111) | data formatting | bytes 18874368 | tf_op jit(solution)/shard_map/reshape | solution.py:72
  530.8 11.0 %copy.200 = f32[96,8,4,768]{3,2,1,0:T(4,128)} copy(f32[96,8,4,768]{3,2,0,1:T(4,128)} %bitcast.316) | data formatting | bytes 18874368 | tf_op jit(solution)/shard_map/transpose | solution.py:73
  541.8 11.1 %reshape.348 = f32[96,24576]{1,0:T(8,128)} reshape(f32[96,8,4,768]{3,2,1,0:T(4,128)} %copy.200) | data formatting | bytes 18874368 | tf_op jit(solution)/shard_map/reshape | solution.py:74
  561.6 4.9 copy.184
  566.5 9.9 %add_add_fusion.2 = f32[1024,768]{1,0:T(8,128)} fusion(f32[1024,768]{1,0:T(8,128)} %copy-done.20, bf16[768,3840]{1,0:T(8,128)(2,1)} %param.12, bf16[1024,1536]{1,0:T(8,128)(2,1)} %bitcast.355, bf16[1024,768]{1,0:T(8,128)(2,1)} %copy.185, f32[1024]{0:T(1024)S(1)} %copy-done.62), kind=kOutput, calls=%fused_computation.72 | convolution fusion | flops 3634888704 | bytes 14553088 | tf_op jit(solution)/shard_map/tk,dk->td/dot_general | solution.py:266
  594.4 62.9 %psum.7 = f32[9,768]{1,0:T(8,128)S(1)} all-reduce(f32[9,768]{1,0:T(8,128)S(1)} %concatenate.40), channel_id=1, replica_groups=mesh['seq'=8,'row'=4] {'seq','row'}, use_global_device_ids=true, to_apply=%region_28.29 | all-reduce | flops 6912 | bytes 55296 | tf_op jit(solution)/shard_map/psum | solution.py:279
  658.5 4.8 fusion.22
  666.0 6.5 reduce-scatter.16.cloned.1.call-done
  674.4 140.2 %reduce-scatter.14.cloned.1.call-done = f32[384,192]{0,1:T(8,128)} async-done(((f32[384,6144]{0,1:T(8,128)}), f32[384,192]{0,1:T(8,128)}) %reduce-scatter.14.cloned.1.call-update) | async-done | bytes 294928 | tf_op jit(solution)/shard_map/reduce_scatter | solution.py:301
  814.7 141.0 %reduce-scatter.12.cloned.1.call-done = f32[96,768]{1,0:T(8,128)} async-done(((f32[96,24576]{1,0:T(8,128)}), f32[96,768]{1,0:T(8,128)}) %reduce-scatter.12.cloned.1.call-update) | async-done | bytes 294928 | tf_op jit(solution)/shard_map/reduce_scatter | solution.py:295
  (312 shorter events, 158.7 us)
Async XLA Ops:
  7.2 150.0 %copy-start = (bf16[768,768]{1,0:T(8,128)(2,1)S(1)}, bf16[768,768]{1,0:T(8,128)(2,1)}, u32[]{:S(2)}) copy-start(bf16[768,768]{1,0:T(8,128)(2,1)} %param.13) | copy-start | bytes 3538948
  7.2 101.5 %all-gather.2.cloned.1.call-start = ((), (), s32[]{:S(2)}) async-start(), calls=%async_computation.5 | async-start | bytes 7077888 | tf_op jit(solution)/shard_map/all_gather | solution.py:125
  9.6 5.0 collective-permute-start.2
  14.1 22.5 %copy-start.40 = (f32[768]{0:T(1024)}, f32[768]{0:T(1024)S(1)}, u32[]{:S(2)}) copy-start(f32[768]{0:T(1024)S(1)} %get-tuple-element.48) | copy-start | bytes 9220
  14.1 22.5 %copy-start.42 = (f32[768]{0:T(1024)}, f32[768]{0:T(1024)S(1)}, u32[]{:S(2)}) copy-start(f32[768]{0:T(1024)S(1)} %get-tuple-element.49) | copy-start | bytes 9220
  14.1 22.5 %copy-start.44 = (f32[768]{0:T(1024)}, f32[768]{0:T(1024)S(1)}, u32[]{:S(2)}) copy-start(f32[768]{0:T(1024)S(1)} %get-tuple-element.50) | copy-start | bytes 9220
  14.1 22.5 %copy-start.46 = (f32[768]{0:T(1024)}, f32[768]{0:T(1024)S(1)}, u32[]{:S(2)}) copy-start(f32[768]{0:T(1024)S(1)} %get-tuple-element.51) | copy-start | bytes 9220
  14.1 22.5 %copy-start.48 = (f32[768]{0:T(1024)}, f32[768]{0:T(1024)S(1)}, u32[]{:S(2)}) copy-start(f32[768]{0:T(1024)S(1)} %get-tuple-element.52) | copy-start | bytes 9220
  40.6 379.1 %reduce-scatter.10.cloned.1.call-start = ((), (), s32[]{:S(2)}) async-start(), calls=%async_computation.6 | async-start | bytes 7077888 | tf_op jit(solution)/shard_map/reduce_scatter | solution.py:230
  49.8 16.6 %collective-permute-start = (bf16[8,64,1536]{2,1,0:T(8,128)(2,1)}, bf16[8,64,1536]{2,1,0:T(8,128)(2,1)}, u32[]{:S(2)}, u32[]{:S(2)}) collective-permute-start(bf16[8,64,1536]{2,1,0:T(8,128)(2,1)} %get-tuple-element.69), channel_id=1, source_target_pairs={{0,4},{4,8},{8,12},{12,16},{16,20},{20,24},{24,28},{1,5},{5,9},{9,... | collective-permute-start | bytes 4718600 | tf_op jit(solution)/shard_map/ppermute | solution.py:25
  55.7 10.7 %collective-permute-start.1 = (bf16[8,64,1536]{2,1,0:T(8,128)(2,1)}, bf16[8,64,1536]{2,1,0:T(8,128)(2,1)}, u32[]{:S(2)}, u32[]{:S(2)}) collective-permute-start(bf16[8,64,1536]{2,1,0:T(8,128)(2,1)} %get-tuple-element.70), channel_id=1, source_target_pairs={{4,0},{8,4},{12,8},{16,12},{20,16},{24,20},{28,24},{5,1},{9,5},{13... | collective-permute-start | bytes 4718600 | tf_op jit(solution)/shard_map/ppermute | solution.py:26
  65.8 58.4 %copy-start.4 = (bf16[8,128,768]{1,2,0:T(8,128)(2,1)}, bf16[8,128,768]{1,2,0:T(8,128)(2,1)S(1)}, u32[]{:S(2)}) copy-start(bf16[8,128,768]{1,2,0:T(8,128)(2,1)S(1)} %copy.149) | copy-start | bytes 4718596
  66.0 103.2 %copy-start.53 = (f32[768]{0:T(1024)}, f32[768]{0:T(1024)S(1)}, u32[]{:S(2)}) copy-start(f32[768]{0:T(1024)S(1)} %get-tuple-element.56) | copy-start | bytes 9220
  66.0 143.5 %copy-start.51 = (f32[768]{0:T(1024)}, f32[768]{0:T(1024)S(1)}, u32[]{:S(2)}) copy-start(f32[768]{0:T(1024)S(1)} %get-tuple-element.124) | copy-start | bytes 9220
  129.5 12.8 %copy-start.2 = (f32[8,12,128,256]{3,2,1,0:T(8,128)}, f32[8,12,128,256]{3,2,1,0:T(8,128)S(1)}, u32[]{:S(2)}) copy-start(f32[8,12,128,256]{3,2,1,0:T(8,128)S(1)} %get-tuple-element.112) | copy-start | bytes 37748740
  129.5 12.8 %copy-start.23 = (bf16[8,256,768]{1,2,0:T(8,128)(2,1)S(1)}, bf16[8,256,768]{1,2,0:T(8,128)(2,1)}, u32[]{:S(2)}) copy-start(bf16[8,256,768]{1,2,0:T(8,128)(2,1)} %copy.173) | copy-start | bytes 9437188
  157.3 11.8 %slice-start.3 = ((s8[4718592]{0:T(1024)(128)(4,1)}), s8[4194304]{0:T(1024)(128)(4,1)S(1)}, s32[]{:S(2)}) async-start(s8[4718592]{0:T(1024)(128)(4,1)} %bitcast.375), calls=%async_computation.14 | async-start | bytes 8388608
  158.9 50.6 %copy-start.6 = (f32[1024,768]{1,0:T(8,128)}, f32[1024,768]{1,0:T(8,128)S(1)}, u32[]{:S(2)}) copy-start(f32[1024,768]{1,0:T(8,128)S(1)} %get-tuple-element.114) | copy-start | bytes 9437188
  158.9 50.6 %copy-start.36 = (f32[1024]{0:T(1024)}, f32[1024]{0:T(1024)S(1)}, u32[]{:S(2)}) copy-start(f32[1024]{0:T(1024)S(1)} %broadcast_multiply_fusion.2) | copy-start | bytes 12292
  159.5 50.1 %copy-start.38 = (f32[1024]{0:T(1024)}, f32[1024]{0:T(1024)S(1)}, u32[]{:S(2)}) copy-start(f32[1024]{0:T(1024)S(1)} %fusion.96) | copy-start | bytes 12292
  160.4 8.8 slice-start.4
  180.3 17.9 %copy-start.31 = (f32[1024,768]{1,0:T(8,128)}, f32[1024,768]{1,0:T(8,128)S(1)}, u32[]{:S(2)}) copy-start(f32[1024,768]{1,0:T(8,128)S(1)} %get-tuple-element.60) | copy-start | bytes 9437188
  180.3 17.9 %copy-start.68 = (f32[1024]{0:T(1024)}, f32[1024]{0:T(1024)S(1)}, u32[]{:S(2)}) copy-start(f32[1024]{0:T(1024)S(1)} %negate_multiply_fusion.1) | copy-start | bytes 12292
  198.2 11.3 %copy-start.24 = (bf16[1024,3072]{1,0:T(8,128)(2,1)}, bf16[1024,3072]{1,0:T(8,128)(2,1)S(1)}, u32[]{:S(2)}) copy-start(bf16[1024,3072]{1,0:T(8,128)(2,1)S(1)} %add_convert_fusion) | copy-start | bytes 18874372
  211.0 82.4 %copy-start.61 = (f32[1024]{0:T(1024)}, f32[1024]{0:T(1024)S(1)}, u32[]{:S(2)}) copy-start(f32[1024]{0:T(1024)S(1)} %negate_multiply_fusion) | copy-start | bytes 12292
  218.7 19.5 %slice-start = ((s8[12582912]{0:T(1024)(128)(4,1)}), s8[4194304]{0:T(1024)(128)(4,1)S(1)}, s32[]{:S(2)}) async-start(s8[12582912]{0:T(1024)(128)(4,1)} %bitcast.304), calls=%async_computation.11 | async-start | bytes 8388608
  218.7 19.5 %slice-start.1 = ((s8[12582912]{0:T(1024)(128)(4,1)}), s8[4194304]{0:T(1024)(128)(4,1)S(1)}, s32[]{:S(2)}) async-start(s8[12582912]{0:T(1024)(128)(4,1)} %bitcast.304), calls=%async_computation.12 | async-start | bytes 8388608
  226.2 12.0 %slice-start.2 = ((s8[12582912]{0:T(1024)(128)(4,1)}), s8[4194304]{0:T(1024)(128)(4,1)S(1)}, s32[]{:S(2)}) async-start(s8[12582912]{0:T(1024)(128)(4,1)} %bitcast.304), calls=%async_computation.13 | async-start | bytes 8388608
  226.3 12.0 %copy-start.28 = (bf16[96,8,8,128]{3,2,1,0:T(8,128)(2,1)S(1)}, bf16[96,8,8,128]{3,2,1,0:T(8,128)(2,1)}, u32[]{:S(2)}) copy-start(bf16[96,8,8,128]{3,2,1,0:T(8,128)(2,1)} %copy-done.27) | copy-start | bytes 4718596
  254.1 21.9 %copy-start.5 = (bf16[8,128,768]{1,2,0:T(8,128)(2,1)S(1)}, bf16[8,128,768]{1,2,0:T(8,128)(2,1)}, u32[]{:S(2)}) copy-start(bf16[8,128,768]{1,2,0:T(8,128)(2,1)} %copy-done.4) | copy-start | bytes 4718596
  290.2 286.2 %reduce-scatter.18.cloned.1.call-start = ((), (), s32[]{:S(2)}) async-start(), calls=%async_computation.10 | async-start | bytes 3244032
  333.2 39.6 %copy-start.35 = (bf16[96,8,8,128]{3,1,2,0:T(8,128)(2,1)S(1)}, bf16[96,8,8,128]{3,1,2,0:T(8,128)(2,1)}, u32[]{:S(2)}) copy-start(bf16[96,8,8,128]{3,1,2,0:T(8,128)(2,1)} %copy.280) | copy-start | bytes 4718596
  337.7 56.6 %collective-permute-start.4 = (bf16[8,64,1536]{2,1,0:T(8,128)(2,1)}, bf16[8,64,1536]{2,1,0:T(8,128)(2,1)}, u32[]{:S(2)}, u32[]{:S(2)}) collective-permute-start(bf16[8,64,1536]{2,1,0:T(8,128)(2,1)} %copy.182), channel_id=1, source_target_pairs={{4,0},{8,4},{12,8},{16,12},{20,16},{24,20},{28,24},{5,1},{9,5},{13... | collective-permute-start | bytes 4718600 | tf_op jit(solution)/shard_map/ppermute | solution.py:34
  339.0 59.4 %collective-permute-start.3 = (bf16[8,64,1536]{2,1,0:T(8,128)(2,1)}, bf16[8,64,1536]{2,1,0:T(8,128)(2,1)}, u32[]{:S(2)}, u32[]{:S(2)}) collective-permute-start(bf16[8,64,1536]{2,1,0:T(8,128)(2,1)} %copy.180), channel_id=1, source_target_pairs={{0,4},{4,8},{8,12},{12,16},{16,20},{20,24},{24,28},{1,5},{5,9},{9,... | collective-permute-start | bytes 4718600 | tf_op jit(solution)/shard_map/ppermute | solution.py:34
  381.5 290.9 %reduce-scatter.16.cloned.1.call-start = ((), (), s32[]{:S(2)}) async-start(), calls=%async_computation.9 | async-start | bytes 16220160
  402.5 10.1 %copy-start.26 = (bf16[8,12,64,128]{3,2,1,0:T(8,128)(2,1)S(1)}, bf16[8,12,64,128]{3,2,1,0:T(8,128)(2,1)}, u32[]{:S(2)}) copy-start(bf16[8,12,64,128]{3,2,1,0:T(8,128)(2,1)} %multiply_convert_fusion.4) | copy-start | bytes 4718596
  402.5 10.1 %copy-start.34 = (bf16[8,128,768]{2,1,0:T(8,128)(2,1)S(1)}, bf16[8,128,768]{2,1,0:T(8,128)(2,1)}, u32[]{:S(2)}) copy-start(bf16[8,128,768]{2,1,0:T(8,128)(2,1)} %param.10) | copy-start | bytes 4718596
  412.6 7.1 copy-start.9
  412.6 7.1 copy-start.11
  412.6 7.1 copy-start.13
  412.6 7.1 copy-start.15
  412.6 7.1 copy-start.41
  412.6 7.1 copy-start.43
  412.6 7.1 copy-start.45
  482.6 332.1 %reduce-scatter.14.cloned.1.call-start = ((), (), s32[]{:S(2)}) async-start(), calls=%async_computation.8 | async-start | bytes 9732096 | tf_op jit(solution)/shard_map/reduce_scatter | solution.py:301
  505.5 450.2 %reduce-scatter.12.cloned.1.call-start = ((), (), s32[]{:S(2)}) async-start(), calls=%async_computation.7 | async-start | bytes 9732096 | tf_op jit(solution)/shard_map/reduce_scatter | solution.py:295
  593.0 65.5 %collective-permute-start.5 = (bf16[8,2,768]{2,0,1:T(8,128)(2,1)S(1)}, bf16[8,2,768]{2,0,1:T(8,128)(2,1)S(1)}, u32[]{:S(2)}, u32[]{:S(2)}) collective-permute-start(bf16[8,2,768]{2,0,1:T(8,128)(2,1)S(1)} %slice.310), channel_id=1, source_target_pairs={{4,0},{8,4},{12,8},{16,12},{20,16},{24,20},{28,24},{5,1},{9,5},{13... | collective-permute-start | bytes 73736 | tf_op jit(solution)/shard_map/ppermute | solution.py:34
  658.5 297.2 %copy-start.1 = (bf16[768,768]{1,0:T(8,128)(2,1)S(1)}, bf16[768,768]{1,0:T(8,128)(2,1)}, u32[]{:S(2)}) copy-start(bf16[768,768]{1,0:T(8,128)(2,1)} %param.13) | copy-start | bytes 3538948
  (42 other events, 153.1 us)
Sparse Core Ops, SparseCore 0:
  40.7 67.9 all-gather.1
  290.3 96.2 reduce-scatter.9
  392.9 101.5 reduce-scatter.17
  501.5 170.9 reduce-scatter.15
  679.8 134.8 reduce-scatter.13
  821.0 134.6 reduce-scatter.11
where the time goes:
time: 972 us; the launch traced here: 963 us
  waiting for transfers between devices  305 us (31%)
  local copies, waits for them, and re-layouts  240 us (25%)
  matrix products  202 us (21%)
  other arithmetic  90.9 us (9%)
  blocking collectives  62.9 us (6%)
  starting transfers between devices  46.3 us (5%)
  between operations  15.7 us (2%)
    reduce_scatter x1, waiting for transfers between devices, body(): lax.psum_scatter(tile_order(w_up_grad, seq_count, row_count), ('seq', 'ro...  141 us
    reduce_scatter x1, waiting for transfers between devices, body(): lax.psum_scatter(tile_order(w_down_grad, seq_count, row_count), ('seq', '...  140 us
    psum x1, blocking collectives, body(): small_sum = lax.psum(small_stack, ('seq', 'row'))  62.9 us
    unnamed x181, local copies, waits for them, and re-layouts  55.8 us
    ppermute x4, starting transfers between devices, passed_along(): return lax.ppermute(block, axis, route)  38.8 us
    reshape x2, local copies, waits for them, and re-layouts, tile_order(): grad.reshape(seq_count, first // seq_count, row_count, second // row_count)  29.8 us
    convert_element_type x1, other arithmetic, body(): near_dscore = (near_prob * (near_dprob - row_dot)).astype(jnp.bfloat16)  21.9 us
  transfers between devices with their start and end apart: 12, of which 4 were waited for; matrix products, arithmetic and copies ran while one was open for 33% of the time, Pallas kernels for 0%

commit v1 on v0

v1 whole, which is shorter than its diff:
```python
import functools

import jax
import jax.numpy as jnp
from jax import lax
from jax.experimental import pallas as pl
from jax.experimental.pallas import tpu as pltpu
from jax.sharding import PartitionSpec as P

HEADS = 12
HEAD = 64
WIN = 128
KER = 5
STR = 4
PAIRS = HEADS // 2

EPSILON = 1e-05
ROOT_HALF = 0.7071067811865476
INV_ROOT_2PI = 0.3989422804014327
NEG_LARGE = -1e30
BF = jnp.bfloat16
F32 = jnp.float32
MB = 1 << 20


def dot(a, b, ca=1, cb=0):
    return lax.dot_general(a, b, (((ca,), (cb,)), ((), ())), preferred_element_type=F32)


def passed_along(block, axis, distance):
    devices = range(lax.axis_size(axis))
    route = [(i - distance, i) for i in devices if i - distance in devices]
    return lax.ppermute(block, axis, route)


def tap_select(seg_row, half, pooled_local):
    width = seg_row.shape[1]
    shape = (KER * pooled_local, width)
    rows = lax.broadcasted_iota(jnp.int32, shape, 0)
    cols = lax.broadcasted_iota(jnp.int32, shape, 1)
    tap = rows // pooled_local
    centre = half + STR * (rows - tap * pooled_local)
    seg = jnp.broadcast_to(seg_row, shape)
    centre_seg = jnp.sum(jnp.where(cols == centre, seg, 0), axis=1, keepdims=True)
    hit = (cols == centre + tap - KER // 2) & (seg == centre_seg)
    return jnp.where(hit, 1.0, 0.0).astype(BF)


def pool_kernel(half, tok_ref, seg_ref, ker_ref, out_ref):
    pooled_local = out_ref.shape[1]
    picked = dot(tap_select(seg_ref[0], half, pooled_local), tok_ref[0])
    total = picked[:pooled_local] * ker_ref[0:1]
    for t in range(1, KER):
        total = total + picked[t * pooled_local : (t + 1) * pooled_local] * ker_ref[t : t + 1]
    out_ref[0] = total.astype(BF)


def attend_kernel(half, tok_ref, pool_ref, qseg_ref, kseg_ref, w_ref, q_ref, k_ref, v_ref, p_ref, att_ref):
    shard = q_ref.shape[1]
    width = tok_ref.shape[2]
    near = shard + 2 * half
    keys = k_ref.shape[1]
    tok = tok_ref[0]
    own = tok_ref[0, half : half + shard]
    q_ref[0] = (dot(own, w_ref[:, :width]) * HEAD ** (-0.5)).astype(BF)
    k_ref[0, :near] = dot(tok, w_ref[:, width : 2 * width]).astype(BF)
    v_ref[0, :near] = dot(tok, w_ref[:, 2 * width : 3 * width]).astype(BF)
    k_ref[0, near:] = dot(pool_ref[0], w_ref[:, 3 * width : 4 * width]).astype(BF)
    v_ref[0, near:] = dot(pool_ref[0], w_ref[:, 4 * width :]).astype(BF)

    key_seg = jnp.transpose(jnp.broadcast_to(kseg_ref[0], (shard, keys)))
    shape = (keys, shard)
    row = lax.broadcasted_iota(jnp.int32, shape, 0)
    col = lax.broadcasted_iota(jnp.int32, shape, 1)
    inside = (row >= near) | ((row >= col) & (row - col <= 2 * half))
    kept = inside & (key_seg == jnp.broadcast_to(qseg_ref[0], shape))
    bias = jnp.where(kept, 0.0, NEG_LARGE)
    bias = jnp.concatenate([bias, bias], axis=1)
    lane = lax.broadcasted_iota(jnp.int32, (shard, 2 * HEAD), 1)
    even = lane < HEAD
    for j in range(PAIRS):
        cols = slice(2 * HEAD * j, 2 * HEAD * (j + 1))
        qp = q_ref[0, :, cols]
        zero = jnp.zeros_like(qp)
        stacked = jnp.concatenate([jnp.where(even, qp, zero), jnp.where(even, zero, qp)], axis=0)
        scores = dot(k_ref[0, :, cols], stacked, 1, 1) + bias
        top = jnp.max(scores, axis=0, keepdims=True)
        terms = jnp.exp(scores - top)
        prob = (terms * (1.0 / jnp.sum(terms, axis=0, keepdims=True))).astype(BF)
        p_ref[0, j] = prob
        mixed = dot(v_ref[0, :, cols], prob, 0, 0)
        mixed = jnp.concatenate([mixed[:HEAD, :shard], mixed[HEAD:, shard:]], axis=0)
        att_ref[0, :, cols] = jnp.transpose(mixed).astype(BF)


def mlp_kernel(
    tok_ref, att_ref, cot_ref, wo_ref, wu_ref, wd_ref, gain_ref, bias_ref,
    out_ref, act_ref, upg_ref, n1_ref, r2_ref, g1_ref, g1b_ref, da_ref, dsum_ref, small_ref,
    slope,
):
    hidden = wu_ref.shape[1]
    chunk = 512
    gain_a, gain_b = gain_ref[0:1], gain_ref[1:2]

    def mean(x):
        return jnp.mean(x, axis=-1, keepdims=True)

    resid = tok_ref[...].astype(F32) + dot(att_ref[...], wo_ref[...])
    centred = resid - mean(resid)
    rstd_a = lax.rsqrt(mean(centred * centred) + EPSILON)
    hat_a = centred * rstd_a
    normed = hat_a * gain_a + bias_ref[0:1]
    low = normed.astype(BF)
    n1_ref[...] = low
    total = normed
    for c in range(0, hidden, chunk):
        up = dot(low, wu_ref[:, c : c + chunk])
        half_cdf = 0.5 * (1.0 + lax.erf(up * ROOT_HALF))
        act = (up * half_cdf).astype(BF)
        act_ref[:, c : c + chunk] = act
        slope[:, c : c + chunk] = half_cdf + up * (INV_ROOT_2PI * jnp.exp(-0.5 * up * up))
        total = total + dot(act, wd_ref[c : c + chunk, :])
    centred = total - mean(total)
    rstd_b = lax.rsqrt(mean(centred * centred) + EPSILON)
    hat_b = centred * rstd_b
    out_ref[...] = (hat_b * gain_b + bias_ref[1:2]).astype(BF)
    g = cot_ref[...].astype(F32)
    gain_two = jnp.sum(g * hat_b, axis=0, keepdims=True)
    bias_two = jnp.sum(g, axis=0, keepdims=True)
    e = g * gain_b
    grad = rstd_b * (e - mean(e) - hat_b * mean(e * hat_b))
    grad_low = grad.astype(BF)
    r2_ref[...] = grad_low
    for c in range(0, hidden, chunk):
        up_grad = (dot(grad_low, wd_ref[c : c + chunk, :], 1, 1) * slope[:, c : c + chunk]).astype(BF)
        upg_ref[:, c : c + chunk] = up_grad
        grad = grad + dot(up_grad, wu_ref[:, c : c + chunk], 1, 1)
    gain_one = jnp.sum(grad * hat_a, axis=0, keepdims=True)
    bias_one = jnp.sum(grad, axis=0, keepdims=True)
    e = grad * gain_a
    resid_grad = rstd_a * (e - mean(e) - hat_a * mean(e * hat_a))
    g1_ref[...] = resid_grad
    resid_low = resid_grad.astype(BF)
    g1b_ref[...] = resid_low
    att_grad = dot(resid_low, wo_ref[...], 1, 1).astype(BF)
    da_ref[...] = att_grad
    prod = att_grad.astype(F32) * att_ref[...].astype(F32)
    high = prod.astype(BF)
    rest = (prod - high.astype(F32)).astype(BF)
    heads = dsum_ref.shape[0]
    width = prod.shape[1]
    head_row = lax.broadcasted_iota(jnp.int32, (heads, width), 0)
    head_col = lax.broadcasted_iota(jnp.int32, (heads, width), 1) // HEAD
    pick = jnp.where(head_row == head_col, 1.0, 0.0).astype(BF)
    dsum_ref[...] = dot(pick, high, 1, 1) + dot(pick, rest, 1, 1)

    @pl.when(pl.program_id(0) == 0)
    def _():
        small_ref[...] = jnp.zeros_like(small_ref)

    small_ref[0:4] += jnp.concatenate([gain_one, gain_two, bias_one, bias_two], axis=0)


def attend_back_kernel(
    half, q_ref, k_ref, v_ref, p_ref, da_ref, dsum_ref, w_ref,
    dq_ref, dk_ref, dv_ref, dtok_ref, dpool_ref,
):
    shard = q_ref.shape[1]
    width = q_ref.shape[2]
    near = shard + 2 * half
    lane = lax.broadcasted_iota(jnp.int32, (shard, 2 * HEAD), 1)
    even = lane < HEAD

    def stack(pair):
        zero = jnp.zeros_like(pair)
        return jnp.concatenate([jnp.where(even, pair, zero), jnp.where(even, zero, pair)], axis=0)

    for j in range(PAIRS):
        cols = slice(2 * HEAD * j, 2 * HEAD * (j + 1))
        queries = stack(q_ref[0, :, cols])
        grads = stack(da_ref[0, :, cols])
        keys = k_ref[0, :, cols]
        prob = p_ref[0, j]
        dprob = dot(v_ref[0, :, cols], grads, 1, 1)
        row_dot = jnp.concatenate([dsum_ref[2 * j : 2 * j + 1], dsum_ref[2 * j + 1 : 2 * j + 2]], axis=1)
        dscore = (prob.astype(F32) * (dprob - row_dot)).astype(BF)
        dv_ref[0, :, cols] = dot(prob, grads).astype(BF)
        dk_ref[0, :, cols] = dot(dscore, queries).astype(BF)
        mixed = dot(keys, dscore, 0, 0)
        mixed = jnp.concatenate([mixed[:HEAD, :shard], mixed[HEAD:, shard:]], axis=0)
        dq_ref[0, :, cols] = (jnp.transpose(mixed) * HEAD ** (-0.5)).astype(BF)
    dtok_ref[0] = dot(dk_ref[0, :near], w_ref[:, width : 2 * width], 1, 1) + dot(
        dv_ref[0, :near], w_ref[:, 2 * width : 3 * width], 1, 1
    )
    dtok_ref[0, half : half + shard] += dot(dq_ref[0], w_ref[:, :width], 1, 1)
    dpool_ref[0] = (
        dot(dk_ref[0, near:], w_ref[:, 3 * width : 4 * width], 1, 1)
        + dot(dv_ref[0, near:], w_ref[:, 4 * width :], 1, 1)
    ).astype(BF)


def pool_back_kernel(half, tok_ref, seg_ref, ker_ref, dpool_ref, dtok_ref, g1_ref, left_ref, right_ref, out_ref, rim_ref, small_ref):
    shard = out_ref.shape[1]
    pooled_local = dpool_ref.shape[1]
    select = tap_select(seg_ref[0], half, pooled_local)
    picked = dot(select, tok_ref[0])
    grad = dpool_ref[0].astype(F32)
    terms, kernel_rows = [], []
    for t in range(KER):
        terms.append((grad * ker_ref[t : t + 1]).astype(BF))
        kernel_rows.append(
            jnp.sum(grad * picked[t * pooled_local : (t + 1) * pooled_local], axis=0, keepdims=True)
        )
    spread = dot(select, jnp.concatenate(terms, axis=0), 0, 0)
    rim_ref[0] = spread[half - 8 : half].astype(BF)
    total = g1_ref[0] + dtok_ref[0, half : half + shard] + spread[half : half + shard]
    out_ref[0] = total
    out_ref[0, :half] += left_ref[0].astype(F32)
    out_ref[0, shard - half :] += right_ref[0].astype(F32)

    @pl.when(pl.program_id(0) == 0)
    def _():
        small_ref[...] = jnp.zeros_like(small_ref)

    small_ref[0:KER] += jnp.concatenate(kernel_rows, axis=0)


def tile_order(grad, seq_count, row_count):
    first, second = grad.shape
    tiles = grad.reshape(seq_count, first // seq_count, row_count, second // row_count)
    tiles = tiles.transpose(0, 2, 1, 3)
    return tiles.reshape(seq_count * row_count * (first // seq_count), second // row_count)


def body(tokens, segment_ids, w_in, w_out, w_up, w_down, conv_kernel, norm_gain, norm_bias, cotangent):
    rows, shard, width = tokens.shape
    half = WIN // 2
    pooled_local = shard // STR
    near = shard + 2 * half
    count = rows * shard
    hidden = w_up.shape[1]
    seq_count = lax.axis_size("seq")
    row_count = lax.axis_size("row")
    seq_start = lax.axis_index("seq") * shard
    keys = near + pooled_local * seq_count

    own_seg = lax.dynamic_slice_in_dim(segment_ids, seq_start, shard, 1)
    padded_seg = jnp.pad(segment_ids, ((0, 0), (half, half)), constant_values=-1)
    window_seg = lax.dynamic_slice_in_dim(padded_seg, seq_start, near, 1)
    key_seg = jnp.concatenate([window_seg, segment_ids[:, ::STR]], axis=1)
    own_seg = own_seg[:, None]
    key_seg = key_seg[:, None]
    window_seg = window_seg[:, None]

    before = passed_along(tokens[:, shard - half :], "seq", 1)
    after = passed_along(tokens[:, :half], "seq", -1)
    tok_ext = jnp.concatenate([before, tokens, after], axis=1)

    def row_spec(*tail):
        return pl.BlockSpec((1,) + tail, lambda r: (r,) + (0,) * len(tail))

    def whole_spec(*dims):
        return pl.BlockSpec(dims, lambda r: (0,) * len(dims), pipeline_mode=pl.Buffered(1))

    def struct(*dims, dtype=BF):
        return jax.ShapeDtypeStruct(dims, dtype)

    def params(limit):
        return pltpu.CompilerParams(dimension_semantics=("arbitrary",), vmem_limit_bytes=limit * MB)

    pooled = pl.pallas_call(
        functools.partial(pool_kernel, half),
        out_shape=struct(rows, pooled_local, width),
        grid=(rows,),
        in_specs=[row_spec(near, width), row_spec(1, near), whole_spec(KER, width)],
        out_specs=row_spec(pooled_local, width),
        compiler_params=params(32),
        name="pool",
    )(tok_ext, window_seg, conv_kernel)
    pooled_all = lax.all_gather(pooled, "seq", axis=1, tiled=True)
    far = pooled_all.shape[1]

    q, k_all, v_all, prob, attended = pl.pallas_call(
        functools.partial(attend_kernel, half),
        out_shape=(
            struct(rows, shard, width), struct(rows, keys, width), struct(rows, keys, width),
            struct(rows, PAIRS, keys, 2 * shard), struct(rows, shard, width),
        ),
        grid=(rows,),
        in_specs=[
            row_spec(near, width), row_spec(far, width), row_spec(1, shard), row_spec(1, keys),
            whole_spec(*w_in.shape),
        ],
        out_specs=(
            row_spec(shard, width), row_spec(keys, width), row_spec(keys, width),
            row_spec(PAIRS, keys, 2 * shard), row_spec(shard, width),
        ),
        compiler_params=params(56),
        name="attend",
    )(tok_ext, pooled_all, own_seg, key_seg, w_in)

    block = 256
    flat_tokens = tokens.reshape(count, width)
    att_flat = attended.reshape(count, width)
    cot_flat = cotangent.reshape(count, width)

    def tok_spec(cols):
        return pl.BlockSpec((block, cols), lambda i: (i, 0))

    layer_out, act, upg, n1, r2, g1, g1b, att_grad, dsum, norm_sums = pl.pallas_call(
        mlp_kernel,
        out_shape=(
            struct(count, width), struct(count, hidden), struct(count, hidden), struct(count, width),
            struct(count, width), struct(count, width, dtype=F32), struct(count, width), struct(count, width),
            struct(16, count, dtype=F32), struct(8, width, dtype=F32),
        ),
        grid=(count // block,),
        in_specs=[
            tok_spec(width), tok_spec(width), tok_spec(width), whole_spec(*w_out.shape),
            whole_spec(*w_up.shape), whole_spec(*w_down.shape), whole_spec(2, width), whole_spec(2, width),
        ],
        out_specs=(
            tok_spec(width), tok_spec(hidden), tok_spec(hidden), tok_spec(width), tok_spec(width),
            tok_spec(width), tok_spec(width), tok_spec(width),
            pl.BlockSpec((16, block), lambda i: (0, i)), pl.BlockSpec((8, width), lambda i: (0, 0)),
        ),
        scratch_shapes=[pltpu.VMEM((block, hidden), F32)],
        compiler_params=params(56),
        name="mlp",
    )(flat_tokens, att_flat, cot_flat, w_out, w_up, w_down, norm_gain, norm_bias)

    dq, dk, dv, dtok, dpool = pl.pallas_call(
        functools.partial(attend_back_kernel, half),
        out_shape=(
            struct(rows, shard, width), struct(rows, keys, width), struct(rows, keys, width),
            struct(rows, near, width, dtype=F32), struct(rows, far, width),
        ),
        grid=(rows,),
        in_specs=[
            row_spec(shard, width), row_spec(keys, width), row_spec(keys, width),
            row_spec(PAIRS, keys, 2 * shard), row_spec(shard, width),
            pl.BlockSpec((16, shard), lambda r: (0, r)), whole_spec(*w_in.shape),
        ],
        out_specs=(
            row_spec(shard, width), row_spec(keys, width), row_spec(keys, width),
            row_spec(near, width), row_spec(far, width),
        ),
        compiler_params=params(56),
        name="attend_back",
    )(q, k_all, v_all, prob, att_grad.reshape(rows, shard, width), dsum, w_in)

    dpool_own = lax.psum_scatter(dpool, "seq", scatter_dimension=1, tiled=True)
    from_right = passed_along(dtok[:, :half].astype(BF), "seq", -1)
    from_left = passed_along(dtok[:, shard + half :].astype(BF), "seq", 1)

    token_grad, rim, ker_sums = pl.pallas_call(
        functools.partial(pool_back_kernel, half),
        out_shape=(
            struct(rows, shard, width, dtype=F32), struct(rows, 8, width), struct(8, width, dtype=F32),
        ),
        grid=(rows,),
        in_specs=[
            row_spec(near, width), row_spec(1, near), whole_spec(KER, width), row_spec(pooled_local, width),
            row_spec(near, width), row_spec(shard, width), row_spec(half, width), row_spec(half, width),
        ],
        out_specs=(
            row_spec(shard, width), row_spec(8, width), pl.BlockSpec((8, width), lambda r: (0, 0)),
        ),
        compiler_params=params(48),
        name="pool_back",
    )(tok_ext, window_seg, conv_kernel, dpool_own, dtok, g1.reshape(rows, shard, width), from_left, from_right)
    rim_back = passed_along(rim, "seq", -1).astype(F32)
    token_grad = token_grad.at[:, shard - 8 :].add(rim_back)

    def product(a, b):
        return lax.dot_general(
            a.reshape(-1, a.shape[-1]), b.reshape(-1, b.shape[-1]), (((0,), (0,)), ((), ())),
            preferred_element_type=F32,
        ).astype(BF)

    w_in_grad = jnp.concatenate(
        [
            product(tokens, dq), product(tok_ext, dk[:, :near]), product(tok_ext, dv[:, :near]),
            product(pooled_all, dk[:, near:]), product(pooled_all, dv[:, near:]),
        ],
        axis=1,
    )

    def reduced(grad):
        first, second = grad.shape
        tiles = tile_order(grad, seq_count, row_count)
        out = lax.psum_scatter(tiles, ("seq", "row"), scatter_dimension=0, tiled=True)
        return out.astype(F32)

    small_sum = lax.psum(jnp.concatenate([ker_sums[:KER], norm_sums[:4]], axis=0), ("seq", "row"))
    return (
        layer_out.reshape(rows, shard, width),
        token_grad,
        reduced(w_in_grad),
        reduced(product(attended, g1b)),
        reduced(product(n1, upg)),
        reduced(product(act, r2)),
        small_sum[:KER],
        small_sum[KER : KER + 2],
        small_sum[KER + 2 : KER + 4],
    )


def solution(mesh):
    placed = (
        P("row", "seq", None), P("row", None), P(), P(), P(), P(), P(), P(), P(), P("row", "seq", None),
    )
    return jax.shard_map(
        body,
        mesh=mesh,
        in_specs=placed,
        out_specs=(
            P("row", "seq", None), P("row", "seq", None), P("seq", "row"), P("seq", "row"),
            P("seq", "row"), P("seq", "row"), P(), P(), P(),
        ),
        check_vma=False,
    )
```

time: 972 us -> 679 us (0.70)
  matrix products: 202 us -> 43.7 us
  local copies, waits for them, and re-layouts: 240 us -> 85.7 us
  Pallas kernels: 0 us -> 135 us
  other arithmetic: 90.9 us -> 10.4 us
  starting transfers between devices: 46.3 us -> 11.5 us
    dot_general x27 -> x8, matrix products: 202 us -> 43.7 us  [product(): lax.dot_general(a.reshape(-1, a.shape[-1]), b.reshape(-1, b.shape[-1]), (...]
    pallas_call x0 -> x5, Pallas kernels: none -> 135 us  [the longest x1 44.3 us: body(): pl.pallas_call(mlp_kernel, out_shape=(struct(count, width), struct(count,...]
    slice x36 -> x4, local copies, waits for them, and re-layouts: 74.7 us -> 3.98 us  [the longest x1 2.39 us: body(): after = passed_along(tokens[:, :half], 'seq', -1)]
    reduce_scatter x3 -> x4, waiting for transfers between devices: 281 us -> 228 us  [the longest x3 228 us: reduced(): lax.psum_scatter(tiles, ('seq', 'row'), scatter_dimension=0, tiled=True)]
    unnamed x181 -> x33, local copies, waits for them, and re-layouts: 55.8 us -> 22.2 us
    all_gather x1, waiting for transfers between devices: 16.9 us -> 46.1 us  [body(): pooled_all = lax.all_gather(pooled, 'seq', axis=1, tiled=True)]
    ppermute x4 -> x5, starting transfers between devices: 38.8 us -> 11.1 us  [passed_along(): return lax.ppermute(block, axis, route)]
    unnamed x8 -> x7, waiting for transfers between devices: 6.57 us -> 33.7 us
  transfers between devices with their start and end apart: 12 -> 11, of which waited for: 4 -> 5; matrix products, arithmetic and copies ran while one was open for 33% -> 19% of each run, Pallas kernels for 0% -> 7%
where the time goes in v1:
time: 679 us; the launch traced here: 668 us
  waiting for transfers between devices  309 us (46%)
  Pallas kernels  135 us (20%)
  local copies, waits for them, and re-layouts  85.7 us (13%)
  blocking collectives  58.4 us (9%)
  matrix products  43.7 us (6%)
  between operations  14.6 us (2%)
  starting transfers between devices  11.5 us (2%)
  other arithmetic  10.4 us (2%)
    reduce_scatter x3, waiting for transfers between devices, reduced(): lax.psum_scatter(tiles, ('seq', 'row'), scatter_dimension=0, tiled=True)  228 us
    psum x1, blocking collectives, body(): lax.psum(jnp.concatenate([ker_sums[:KER], norm_sums[:4]], axis=0), ('seq'...  58.4 us
    all_gather x1, waiting for transfers between devices, body(): pooled_all = lax.all_gather(pooled, 'seq', axis=1, tiled=True)  46.1 us
    pallas_call x1, Pallas kernels, body(): pl.pallas_call(mlp_kernel, out_shape=(struct(count, width), struct(count,...  44.3 us
    dot_general x8, matrix products, product(): lax.dot_general(a.reshape(-1, a.shape[-1]), b.reshape(-1, b.shape[-1]), (...  43.7 us
    pallas_call x1, Pallas kernels, body(): pl.pallas_call(functools.partial(attend_kernel, half), out_shape=(struct(...  39.1 us
    pallas_call x1, Pallas kernels, body(): pl.pallas_call(functools.partial(attend_back_kernel, half), out_shape=(st...  37.6 us
    unnamed x7, waiting for transfers between devices  33.7 us
  transfers between devices with their start and end apart: 11, of which 5 were waited for; matrix products, arithmetic and copies ran while one was open for 19% of the time, Pallas kernels for 7%

profile of v1, /device:TPU:0, one launch (start us, length us, event | category | flops | bytes accessed | tf_op | source)
XLA Modules:
  0.0 668.4 jit_solution(2827936687211761806)
XLA Ops:
  7.2 2.4 fusion.31
  9.6 3.3 collective-permute-start
  12.9 1.3 collective-permute-start.1
  14.3 1.2 constant_dynamic-update-slice_fusion.2
  15.5 1.5 constant_dynamic-update-slice_fusion.1
  17.0 1.6 collective-permute-done.1
  18.6 1.2 constant_dynamic-update-slice_fusion.tok_ref
  19.8 4.4 pool.1
  25.9 46.1 %all-gather.2.cloned.1.call-done.pool_ref = bf16[8,256,768]{2,1,0:T(8,128)(2,1)} async-done(((bf16[8,32,768]{2,1,0:T(8,128)(2,1)}), bf16[8,256,768]{2,1,0:T(8,128)(2,1)}) %all-gather.2.cloned.1.call-update) | async-done | bytes 3145744 | tf_op jit(solution)/shard_map/all_gather | solution.py:280
  72.0 39.1 %attend.1 = (bf16[8,128,768]{2,1,0:T(8,128)(2,1)}, bf16[8,512,768]{2,1,0:T(8,128)(2,1)}, bf16[8,512,768]{2,1,0:T(8,128)(2,1)}, bf16[8,6,512,256]{3,2,1,0:T(8,128)(2,1)}, bf16[8,128,768]{2,1,0:T(8,128)(2,1)}) custom-call(bf16[8,256,768]{2,1,0:T(8,128)(2,1)} %copy-done, bf16[8,256,768]{2,1,0:T(8,128)(2,1)} %all-gather.2.cloned.1.call-done.pool_ref, ...), custom_call_target="tpu_custom_call" | custom-call | tf_op jit(solution)/shard_map/attend/pallas_call | solution.py:283
  111.0 44.3 %mlp.1 = (bf16[1024,768]{1,0:T(8,128)(2,1)}, bf16[1024,3072]{1,0:T(8,128)(2,1)}, bf16[1024,3072]{1,0:T(8,128)(2,1)}, bf16[1024,768]{1,0:T(8,128)(2,1)}, bf16[102...) custom-call(bf16[1024,768]{1,0:T(8,128)(2,1)} %bitcast.69, ...), custom_call_target="tpu_custom_call" | custom-call | tf_op jit(solution)/shard_map/mlp/pallas_call | solution.py:310
  155.4 2.8 convolution_convert_fusion.2
  158.2 1.4 reshape.110
  159.7 1.4 copy.55
  161.2 37.6 %attend_back.1 = (bf16[8,128,768]{2,1,0:T(8,128)(2,1)}, bf16[8,512,768]{2,1,0:T(8,128)(2,1)}, bf16[8,512,768]{2,1,0:T(8,128)(2,1)}, f32[8,256,768]{2,1,0:T(8,128)}, bf16[8,256,768]{2,1,0:T(8,128)(2,1)}) custom-call(bf16[8,128,768]{2,1,0:T(8,128)(2,1)} %get-tuple-element.46.q_ref, bf16[8,512,768]{2,1,0:T(8,128)(2,1)} %get-tuple-element.47.k_ref, ...), custom_call_target="tpu_custom_call" | custom-call | tf_op jit(solution)/shard_map/attend_back/pallas_call | solution.py:332
  198.8 1.3 copy-done.9
  200.2 9.7 %convolution_convert_fusion = bf16[3072,768]{1,0:T(8,128)(2,1)} fusion(bf16[1024,3072]{1,0:T(8,128)(2,1)} %get-tuple-element.63, bf16[1024,768]{1,0:T(8,128)(2,1)S(1)} %copy-done.9), kind=kOutput, calls=%fused_computation | convolution fusion | flops 4834197504 | bytes 12582912 | tf_op jit(solution)/shard_map/dot_general | solution.py:376
  209.9 6.6 copy.57
  216.5 5.7 copy.68
  222.3 9.0 %copy.66 = bf16[8,4,384,192]{3,2,1,0:T(8,128)(2,1)} copy(bf16[8,4,384,192]{2,0,3,1:T(8,128)(2,1)} %bitcast.68) | data formatting | bytes 9437184
  231.4 1.3 copy-done.8
  232.7 9.6 %convolution_convert_fusion.1 = bf16[768,3072]{1,0:T(8,128)(2,1)} fusion(bf16[1024,768]{1,0:T(8,128)(2,1)S(1)} %copy-done.8, bf16[1024,3072]{1,0:T(8,128)(2,1)} %get-tuple-element.62), kind=kOutput, calls=%fused_computation.1 | convolution fusion | flops 4834197504 | bytes 12582912 | tf_op jit(solution)/shard_map/dot_general | solution.py:376
  242.3 9.7 %reshape.112 = bf16[8,96,4,768]{3,2,1,0:T(4,128)(2,1)} reshape(bf16[768,3072]{1,0:T(8,128)(2,1)} %convolution_convert_fusion.1) | data formatting | bytes 9437184 | tf_op jit(solution)/shard_map/reshape | solution.py:230
  252.0 5.4 copy.56
  257.7 4.5 fusion.29
  262.2 5.8 fusion.16
  268.0 3.7 fusion.19
  271.7 3.7 fusion.22
  275.4 3.9 fusion.25
  279.3 8.4 %copy.53 = bf16[768,3840]{1,0:T(8,128)(2,1)} copy(bf16[768,3840]{0,1:T(8,128)(2,1)} %fusion.25) | data formatting | bytes 11796480 | tf_op jit(solution)/shard_map/concatenate | solution.py:381
  287.7 15.0 %reshape.108 = bf16[8,96,4,960]{3,2,1,0:T(4,128)(2,1)} reshape(bf16[768,3840]{1,0:T(8,128)(2,1)} %copy.53) | data formatting | bytes 11796480 | tf_op jit(solution)/shard_map/reshape | solution.py:230
  302.6 7.8 %copy.54 = bf16[8,4,96,960]{3,2,1,0:T(8,128)(2,1)} copy(bf16[8,4,96,960]{3,1,2,0:T(4,128)(2,1)} %bitcast.63) | data formatting | bytes 11796480 | tf_op jit(solution)/shard_map/transpose | solution.py:231
  310.5 3.1 convert.4
  313.6 1.3 fusion.30
  314.9 1.3 collective-permute-start.3
  316.2 4.0 collective-permute-start.2
  320.2 1.4 convert_element_type.53
  321.7 1.0 copy-done.2
  322.7 9.4 %pool_back.1 = (f32[8,128,768]{2,1,0:T(8,128)}, bf16[8,8,768]{2,1,0:T(8,128)(2,1)S(1)}, f32[8,768]{1,0:T(8,128)S(1)}) custom-call(bf16[8,256,768]{2,1,0:T(8,128)(2,1)S(1)} %copy-done.1, s32[8,1,256]{2,1,0:T(1,128)S(1)} %broadcast_in_dim.9.seg_ref, f32[5,768]{1,0:T(8,128)S(1)} %copy-done.3, bf16[8,32,768]{2,1,0:T(8,128)(2,1)S(1)} %copy-done.2, ...), custom_call_target="tpu_custom_call" | custom-call | tf_op jit(solution)/shard_map/pool_back/pallas_call | solution.py:356
  332.0 1.3 collective-permute-start.4
  333.3 58.4 %psum.7 = f32[9,768]{1,0:T(8,128)S(1)} all-reduce(f32[9,768]{1,0:T(8,128)S(1)} %pad_maximum_fusion), channel_id=1, replica_groups=mesh['seq'=8,'row'=4] {'seq','row'}, use_global_device_ids=true, to_apply=%region_5.6 | all-reduce | flops 6912 | bytes 55296 | tf_op jit(solution)/shard_map/psum | solution.py:395
  392.9 1.7 add_dynamic-update-slice_fusion
  394.6 33.6 %reduce-scatter.16.cloned.1.call-done = bf16[384,192]{1,0:T(8,128)(2,1)} async-done(((bf16[12288,192]{1,0:T(8,128)(2,1)}), bf16[384,192]{1,0:T(8,128)(2,1)}) %reduce-scatter.16.cloned.1.call-update) | async-done | bytes 147472
  428.2 1.1 copy.65
  430.0 109.7 %reduce-scatter.14.cloned.1.call-done = bf16[96,768]{1,0:T(8,128)(2,1)} async-done(((bf16[3072,768]{1,0:T(8,128)(2,1)}), bf16[96,768]{1,0:T(8,128)(2,1)}) %reduce-scatter.14.cloned.1.call-update) | async-done | bytes 147472 | tf_op jit(solution)/shard_map/reduce_scatter | solution.py:392
  539.8 1.6 convert_element_type.55
  541.4 118.2 %reduce-scatter.10.cloned.1.call-done = bf16[96,960]{1,0:T(8,128)(2,1)} async-done(((bf16[3072,960]{1,0:T(8,128)(2,1)}), bf16[96,960]{1,0:T(8,128)(2,1)}) %reduce-scatter.10.cloned.1.call-update) | async-done | bytes 184336 | tf_op jit(solution)/shard_map/reduce_scatter | solution.py:392
  659.6 1.7 convert_element_type.51
  (56 shorter events, 4.2 us)
Async XLA Ops:
  7.2 7.0 %copy-start.6 = (s32[8,1024]{1,0:T(8,128)S(1)}, s32[8,1024]{1,0:T(8,128)}, u32[]{:S(2)}) copy-start(s32[8,1024]{1,0:T(8,128)} %param.13) | copy-start | bytes 98308
  7.2 64.8 %all-gather.2.cloned.1.call-start = ((), (), s32[]{:S(2)}) async-start(), calls=%async_computation.5 | async-start | bytes 3538944 | tf_op jit(solution)/shard_map/all_gather | solution.py:280
  9.6 4.7 collective-permute-start
  12.9 5.7 collective-permute-start.1
  14.3 5.5 copy-start.3
  19.8 52.1 %copy-start = (bf16[8,256,768]{2,1,0:T(8,128)(2,1)}, bf16[8,256,768]{2,1,0:T(8,128)(2,1)S(1)}, u32[]{:S(2)}) copy-start(bf16[8,256,768]{2,1,0:T(8,128)(2,1)S(1)} %constant_dynamic-update-slice_fusion.tok_ref) | copy-start | bytes 9437188
  24.3 295.9 %reduce-scatter.12.cloned.1.call-start = ((), (), s32[]{:S(2)}) async-start(), calls=%async_computation.8 | async-start | bytes 1622016 | tf_op jit(solution)/shard_map/reduce_scatter | solution.py:392
  111.0 44.3 %copy-start.5 = (bf16[8,128,768]{2,1,0:T(8,128)(2,1)S(1)}, bf16[8,128,768]{2,1,0:T(8,128)(2,1)}, u32[]{:S(2)}) copy-start(bf16[8,128,768]{2,1,0:T(8,128)(2,1)} %get-tuple-element.44) | copy-start | bytes 4718596
  161.1 160.5 %reduce-scatter.8.cloned.1.call-start = ((), (), s32[]{:S(2)}) async-start(), calls=%async_computation.6 | async-start | bytes 3538944 | tf_op jit(solution)/shard_map/reduce_scatter | solution.py:352
  198.7 1.4 copy-start.9
  198.8 229.5 %reduce-scatter.16.cloned.1.call-start = ((), (), s32[]{:S(2)}) async-start(), calls=%async_computation.10 | async-start | bytes 6488064
  231.3 1.4 copy-start.8
  231.3 308.5 %reduce-scatter.14.cloned.1.call-start = ((), (), s32[]{:S(2)}) async-start(), calls=%async_computation.9 | async-start | bytes 4866048 | tf_op jit(solution)/shard_map/reduce_scatter | solution.py:392
  257.4 402.2 %reduce-scatter.10.cloned.1.call-start = ((), (), s32[]{:S(2)}) async-start(), calls=%async_computation.7 | async-start | bytes 6488064 | tf_op jit(solution)/shard_map/reduce_scatter | solution.py:392
  257.7 4.5 copy-start.1
  257.7 10.3 %slice-start = ((s8[6291456]{0:T(1024)(128)(4,1)}), s8[4194304]{0:T(1024)(128)(4,1)S(1)}, s32[]{:S(2)}) async-start(s8[6291456]{0:T(1024)(128)(4,1)} %bitcast.78), calls=%async_computation.11 | async-start | bytes 8388608
  262.2 5.8 slice-start.1
  262.2 9.5 %slice-start.2 = ((s8[6291456]{0:T(1024)(128)(4,1)}), s8[4194304]{0:T(1024)(128)(4,1)S(1)}, s32[]{:S(2)}) async-start(s8[6291456]{0:T(1024)(128)(4,1)} %bitcast.80), calls=%async_computation.13 | async-start | bytes 8388608
  268.0 3.7 slice-start.3
  268.0 3.7 copy-start.4
  313.6 6.5 copy-start.7
  314.9 6.7 %collective-permute-start.3 = (bf16[8,64,768]{2,1,0:T(8,128)(2,1)}, bf16[8,64,768]{2,1,0:T(8,128)(2,1)}, u32[]{:S(2)}, u32[]{:S(2)}) collective-permute-start(bf16[8,64,768]{2,1,0:T(8,128)(2,1)} %get-tuple-element.67), channel_id=1, source_target_pairs={{4,0},{8,4},{12,8},{16,12},{20,16},{24,20},{28,24},{5,1},{9,5},{13... | collective-permute-start | bytes 2359304 | tf_op jit(solution)/shard_map/ppermute | solution.py:33
  316.2 5.4 collective-permute-start.2
  321.6 1.0 copy-start.2
  332.0 60.9 %collective-permute-start.4 = (bf16[8,8,768]{2,1,0:T(8,128)(2,1)S(1)}, bf16[8,8,768]{2,1,0:T(8,128)(2,1)S(1)}, u32[]{:S(2)}, u32[]{:S(2)}) collective-permute-start(bf16[8,8,768]{2,1,0:T(8,128)(2,1)S(1)} %get-tuple-element.56), channel_id=1, source_target_pairs={{4,0},{8,4},{12,8},{16,12},{20,16},{24,20},{28,24},{5,1},{9,5},{13... | collective-permute-start | bytes 294920 | tf_op jit(solution)/shard_map/ppermute | solution.py:33
Sparse Core Ops, SparseCore 0:
  24.4 47.5 all-gather.1
  161.2 97.0 reduce-scatter.11
  261.7 45.2 reduce-scatter.7
  313.4 114.7 reduce-scatter.15
  433.6 106.1 reduce-scatter.13
  546.2 113.3 reduce-scatter.9
